TPU v7x, 256 devices: a whole 4x4x8 slice. The times are simulated.
256 devices in a mesh: ia: 4 (over y), ja: 4 (over x), ka: 16 (over z, core).
Axes of the slice: x: 4, y: 4, z: 8, core: 2. Of those that a mesh axis runs over, the one named last changes fastest.
Arguments:
- blocks: bfloat16 [4, 4, 16, 2, 128, 128, 128], P('ia', 'ja', 'ka'), may hold values from -6 to 6
- first_mode_rows: int32 [4, 4, 16, 2], P('ia', 'ja', 'ka'), may hold values from 0 to 15
- second_mode_rows: int32 [4, 4, 16, 2], P('ia', 'ja', 'ka'), may hold values from 0 to 15
- third_mode_rows: int32 [4, 4, 16, 2], P('ia', 'ja', 'ka'), may hold values from 0 to 3
- filled: int32 [4, 4, 16], P('ia', 'ja', 'ka'), may hold values from 1 to 2, as said below
- owner_one: int32 [64], replicated, may hold values from 0 to 63, each once
- owner_two: int32 [64], replicated, may hold values from 0 to 63, each once
- factor_b: float32 [4, 2048, 256], P('ja', ('ia', 'ka'))
- factor_c: float32 [16, 512, 256], P('ka')
Outputs:
- a_new: float32 [4, 2048, 256], P('ia', ('ja', 'ka'))
- b_new: float32 [4, 2048, 256], P('ja', ('ia', 'ka'))
Inputs may be any that keep to these rules, and one draw needn't show every extreme that they name: Number of nonempty slots of a grid cell; at least one cell has all 2 slots filled. Slots at or beyond this count hold data that is not part of the tensor.
All inputs are finite; a program needn't handle non-finite values.
Results may differ from a plain program's by a relative error of at most 0.0039.
The roundings to bfloat16 on the way count: a program that leaves them out, or rounds other values in their place, can miss the bound.
Values may be sent and summed in bfloat16 or wider, within the bound.
A program may use at most 128 MiB of HBM per device.

v0:
```python
import jax
import jax.numpy as jnp
from jax import lax
from jax.sharding import PartitionSpec as P

EPS = 1e-06


def solve_rows(gram, rows):
    lower = jnp.linalg.cholesky(gram)
    return jax.scipy.linalg.cho_solve((lower, True), rows.T).T


def add_rows(accum, start, contrib):
    current = lax.dynamic_slice_in_dim(accum, start, contrib.shape[0], 0)
    return lax.dynamic_update_slice_in_dim(accum, current + contrib, start, 0)


def batched_sum(inner, weights):
    summed = lax.dot_general(
        inner,
        weights.astype(jnp.float32),
        (((1,), (0,)), ((2,), (1,))),
        precision=lax.Precision.HIGHEST,
        preferred_element_type=jnp.float32,
    )
    return summed.T


def to_logical(stored, owner, piece_rows):
    return stored.reshape(-1, piece_rows, stored.shape[1])[owner].reshape(stored.shape)


def to_stored(logical, owner, piece_rows):
    positions = jnp.arange(owner.shape[0], dtype=jnp.int32)
    inverse = jnp.sum(
        jnp.where(owner[None, :] == positions[:, None], positions[None, :], 0), axis=1
    )
    return logical.reshape(-1, piece_rows, logical.shape[1])[inverse].reshape(logical.shape)


def keep_same(value):
    return value


def partial_value(function, slot):

    def applied(value):
        return function(value, slot)

    return applied


def body(
    blocks,
    first_mode_rows,
    second_mode_rows,
    third_mode_rows,
    filled,
    owner_one,
    owner_two,
    factor_b,
    factor_c,
):
    highest = lax.Precision.HIGHEST
    piece_rows = factor_b.shape[1]
    rank_width = factor_b.shape[2]
    block_edge = blocks.shape[-1]
    slot_count = blocks.shape[3]
    total_one = piece_rows * lax.axis_size("ia") * lax.axis_size("ja") * lax.axis_size("ka")
    slab_rows_one = piece_rows * lax.axis_size("ja") * lax.axis_size("ka")
    slab_rows_two = piece_rows * lax.axis_size("ia") * lax.axis_size("ka")
    own_b = factor_b[0]
    own_c = lax.dynamic_slice_in_dim(
        factor_c[0], lax.axis_index(("ia", "ja")) * piece_rows, piece_rows, 0
    )
    local_b = jnp.dot(own_b.T, own_b, precision=highest, preferred_element_type=jnp.float32)
    local_c = jnp.dot(own_c.T, own_c, precision=highest, preferred_element_type=jnp.float32)
    gram_b, gram_c = lax.psum((local_b, local_c), ("ia", "ja", "ka"))
    stored_b = lax.all_gather(factor_b.astype(jnp.bfloat16), ("ia", "ka"), axis=1, tiled=True)[0]
    half_b = to_logical(stored_b, owner_two, piece_rows)
    half_c = factor_c[0].astype(jnp.bfloat16)
    live_count = filled[0, 0, 0]

    def update_one(partial_sum, slot):
        block = blocks[0, 0, 0, slot]
        b_rows = lax.dynamic_slice_in_dim(
            half_b, second_mode_rows[0, 0, 0, slot] * block_edge, block_edge, 0
        )
        c_rows = lax.dynamic_slice_in_dim(
            half_c, third_mode_rows[0, 0, 0, slot] * block_edge, block_edge, 0
        )
        inner = jnp.dot(
            block.reshape(block_edge * block_edge, block_edge),
            c_rows,
            preferred_element_type=jnp.float32,
        )
        inner = inner.reshape(block_edge, block_edge, rank_width)
        contrib = batched_sum(inner, b_rows)
        return add_rows(partial_sum, first_mode_rows[0, 0, 0, slot] * block_edge, contrib)

    partial_one = jnp.zeros((slab_rows_one, rank_width), jnp.float32)
    for slot in range(slot_count):
        partial_one = lax.cond(
            slot < live_count, partial_value(update_one, slot), keep_same, partial_one
        )
    stored_one = to_stored(partial_one, owner_one, piece_rows)
    system_one = gram_b * gram_c
    summed_own = lax.psum_scatter(stored_one, ("ja", "ka"), scatter_dimension=0, tiled=True)
    a_hat = solve_rows(system_one, summed_own)
    squares_a = lax.psum(jnp.sum(a_hat * a_hat, axis=0), ("ia", "ja", "ka"))
    scale_a = jnp.sqrt(squares_a / total_one + EPS)
    a_own = a_hat / scale_a
    local_a = jnp.dot(a_own.T, a_own, precision=highest, preferred_element_type=jnp.float32)
    gram_a = lax.psum(local_a, ("ia", "ja", "ka"))
    stored_a = lax.all_gather(a_own.astype(jnp.bfloat16)[None], ("ja", "ka"), axis=1, tiled=True)[0]
    half_a = to_logical(stored_a, owner_one, piece_rows)

    def update_two(partial_sum, slot):
        block = blocks[0, 0, 0, slot]
        a_rows = lax.dynamic_slice_in_dim(
            half_a, first_mode_rows[0, 0, 0, slot] * block_edge, block_edge, 0
        )
        c_rows = lax.dynamic_slice_in_dim(
            half_c, third_mode_rows[0, 0, 0, slot] * block_edge, block_edge, 0
        )
        inner = lax.dot_general(
            block.reshape(block_edge, block_edge * block_edge),
            a_rows,
            (((0,), (0,)), ((), ())),
            preferred_element_type=jnp.float32,
        )
        inner = inner.reshape(block_edge, block_edge, rank_width)
        contrib = batched_sum(inner, c_rows)
        return add_rows(partial_sum, second_mode_rows[0, 0, 0, slot] * block_edge, contrib)

    partial_two = jnp.zeros((slab_rows_two, rank_width), jnp.float32)
    for slot in range(slot_count):
        partial_two = lax.cond(
            slot < live_count, partial_value(update_two, slot), keep_same, partial_two
        )
    stored_two = to_stored(partial_two, owner_two, piece_rows)
    summed_two = lax.psum_scatter(stored_two, ("ia", "ka"), scatter_dimension=0, tiled=True)
    b_hat = solve_rows(gram_a * gram_c, summed_two)
    squares_b = lax.psum(jnp.sum(b_hat * b_hat, axis=0), ("ia", "ja", "ka"))
    b_own = b_hat / jnp.sqrt(squares_b / total_one + EPS)
    return (a_own[None], b_own[None])


def solution(mesh):
    return jax.shard_map(
        body,
        mesh=mesh,
        in_specs=(
            P("ia", "ja", "ka", None, None, None, None),
            P("ia", "ja", "ka", None),
            P("ia", "ja", "ka", None),
            P("ia", "ja", "ka", None),
            P("ia", "ja", "ka"),
            P(),
            P(),
            P("ja", ("ia", "ka"), None),
            P("ka", None, None),
        ),
        out_specs=(P("ia", ("ja", "ka"), None), P("ja", ("ia", "ka"), None)),
        check_vma=False,
    )
```

profile of v0, /device:TPU:1, one launch (start us, length us, event | category | flops | bytes accessed | tf_op | source)
XLA Modules:
  0.0 827.5 jit_solution(4852424667202017735)
XLA Ops:
  17.5 75.5 %all-gather.4.cloned.1.call-done = bf16[1,2048,256]{2,1,0:T(8,128)(2,1)} async-done(((bf16[1,32,256]{2,1,0:T(8,128)(2,1)}), bf16[1,2048,256]{2,1,0:T(8,128)(2,1)}) %all-gather.4.cloned.1.call-update) | async-done | bytes 1048592 | tf_op jit(solution)/shard_map/all_gather | solution.py:80
  94.8 23.3 %conditional.4 = (f32[2048,256]{1,0:T(8,128)}) conditional(s32[]{:T(128)} %bitcast.41, () %tuple.54, (s32[1,1,1,2]{3,2,1,0:T(1,128)}, bf16[512,256]{1,0:T(8,128)(2,1)S(1)}, bf16[1,1,1,2,128,128,128]{6,5,4,3,2,1,0:T(8,128)(2,1)}, s32[1,1,1,2]{3,2,1,0:T(1,128)}, bf16[2048,256]{1,0:T(8,128)(2,1)S(1)}, /*index=5*/s32[1,1,1,2]{3,2,1,0:T(1,128)}) %tuple.134), branch_computations={%region_6.0_spmd, %region_7.0_spmd} | conditional | flops 1082130432 | bytes 83099928 | solution.py:104
  100.7 6.7 copy.52
  107.6 8.2 multiply_reduce_fusion
  118.1 3.6 gather_fusion.1
  122.1 149.6 %all-reduce.7.cloned.1.call-done = (f32[256,256]{0,1:T(8,128)}, f32[256,256]{0,1:T(8,128)}) async-done(((f32[256,256]{0,1:T(8,128)}, f32[256,256]{0,1:T(8,128)}), (f32[256,256]{0,1:T(8,128)}, f32[256,256]{0,1:T(8,128)})) %all-reduce.7.cloned.1.call-update) | async-done | bytes 524304 | tf_op jit(solution)/shard_map/psum | solution.py:79
  272.9 11.7 %cholesky.130 = f32[128,128]{1,0:T(8,128)S(1)} custom-call(f32[128,128]{1,0:T(8,128)S(1)} %cholesky.194), custom_call_target="Cholesky" | custom-call | tf_op jit(solution)/shard_map/jit(cholesky)/cholesky | solution.py:10
  284.7 9.8 %custom-call.15 = f32[1,128,128]{1,2,0:T(8,128)S(1)} custom-call(f32[1,128,128]{2,1,0:T(8,128)S(1)} %get-tuple-element.155), custom_call_target="InvertDiagBlocksLowerTriangular" | custom-call | tf_op jit(solution)/shard_map/jit(cholesky)/cholesky | solution.py:10
  295.0 11.7 %cholesky.147 = f32[128,128]{1,0:T(8,128)S(1)} custom-call(f32[128,128]{1,0:T(8,128)S(1)} %convolution_subtract_fusion.1), custom_call_target="Cholesky" | custom-call | tf_op jit(solution)/shard_map/jit(cholesky)/cholesky | solution.py:10
  308.8 14.6 %while.4 = (s32[]{:T(128)}, f32[256,256]{1,0:T(8,128)S(1)}, s32[2,2]{1,0:T(2,128)S(1)}, f32[2,128,128]{2,1,0:T(8,128)S(1)}, s32[]{:T(128)}) while((s32[]{:T(128)}, f32[256,256]{1,0:T(8,128)S(1)}, s32[2,2]{1,0:T(2,128)S(1)}, f32[2,128,128]{2,1,0:T(8,128)S(1)}, s32[]{:T(128)}) %tuple.103), condition=%wide.while_cond, body=%wide.while_body.sunk | while | flops 2 | bytes 131181 | solution.py:11
  323.4 19.7 %custom-call.16 = f32[2,128,128]{1,2,0:T(8,128)S(1)} custom-call(f32[2,128,128]{2,1,0:T(8,128)S(1)} %get-tuple-element.124), custom_call_target="InvertDiagBlocksLowerTriangular" | custom-call | tf_op jit(solution)/shard_map/jit(_cho_solve)/triangular_solve | solution.py:11
  345.9 77.9 %psum.37 = f32[256]{0:T(256)S(1)} all-reduce(f32[256]{0:T(256)S(1)} %multiply_reduce_fusion.5), channel_id=1, replica_groups=mesh['ia'=4,'ja'=4,'ka'=16] {'ia','ja','ka'}, use_global_device_ids=true, to_apply=%region_13.16 | all-reduce | flops 256 | bytes 2048 | tf_op jit(solution)/shard_map/psum | solution.py:111
  425.8 71.7 %all-gather.6.cloned.1.call-done = bf16[2048,256]{1,0:T(8,128)(2,1)} async-done(((bf16[32,256]{1,0:T(8,128)(2,1)}), bf16[2048,256]{1,0:T(8,128)(2,1)}) %all-gather.6.cloned.1.call-update) | async-done | bytes 1048592 | tf_op jit(solution)/shard_map/all_gather | solution.py:116
  499.4 23.6 %conditional.6 = (f32[2048,256]{1,0:T(8,128)}) conditional(s32[]{:T(128)} %bitcast.41, () %tuple.57, (s32[1,1,1,2]{3,2,1,0:T(1,128)S(1)}, bf16[2048,256]{1,0:T(8,128)(2,1)S(1)}, bf16[1,1,1,2,128,128,128]{6,5,4,3,2,1,0:T(8,128)(2,1)}, s32[1,1,1,2]{3,2,1,0:T(1,128)S(1)}, bf16[512,256]{1,0:T(8,128)(2,1)S(1)}, ...), branch_computations={%region_15.18_spmd, %region_16.19_spmd} | conditional | flops 1082130432 | bytes 83099800 | solution.py:139
  505.5 6.7 copy.55
  512.4 8.3 multiply_reduce_fusion.2
  523.1 3.7 gather_fusion.3
  526.8 150.8 %all-reduce.5.cloned.1.call-done = f32[256,256]{0,1:T(8,128)} async-done(((f32[256,256]{0,1:T(8,128)}), f32[256,256]{0,1:T(8,128)}) %all-reduce.5.cloned.1.call-update) | async-done | bytes 262160 | tf_op jit(solution)/shard_map/psum | solution.py:115
  678.8 11.7 %cholesky.164 = f32[128,128]{1,0:T(8,128)S(1)} custom-call(f32[128,128]{1,0:T(8,128)S(1)} %cholesky.197), custom_call_target="Cholesky" | custom-call | tf_op jit(solution)/shard_map/jit(cholesky)/cholesky | solution.py:10
  690.6 9.8 %custom-call.17 = f32[1,128,128]{1,2,0:T(8,128)S(1)} custom-call(f32[1,128,128]{2,1,0:T(8,128)S(1)} %get-tuple-element.151), custom_call_target="InvertDiagBlocksLowerTriangular" | custom-call | tf_op jit(solution)/shard_map/jit(cholesky)/cholesky | solution.py:10
  700.9 11.7 %cholesky.181 = f32[128,128]{1,0:T(8,128)S(1)} custom-call(f32[128,128]{1,0:T(8,128)S(1)} %convolution_subtract_fusion), custom_call_target="Cholesky" | custom-call | tf_op jit(solution)/shard_map/jit(cholesky)/cholesky | solution.py:10
  715.2 4.2 while.5
  719.4 19.7 %custom-call.18 = f32[2,128,128]{1,2,0:T(8,128)S(1)} custom-call(f32[2,128,128]{2,1,0:T(8,128)S(1)} %get-tuple-element.125), custom_call_target="InvertDiagBlocksLowerTriangular" | custom-call | tf_op jit(solution)/shard_map/jit(_cho_solve)/triangular_solve | solution.py:11
  742.0 77.3 %psum.39 = f32[256]{0:T(256)S(1)} all-reduce(f32[256]{0:T(256)S(1)} %multiply_reduce_fusion.4), channel_id=1, replica_groups=mesh['ia'=4,'ja'=4,'ka'=16] {'ia','ja','ka'}, use_global_device_ids=true, to_apply=%region_22.25 | all-reduce | flops 256 | bytes 2048 | tf_op jit(solution)/shard_map/psum | solution.py:145
  (117 shorter events, 50.5 us)
Async XLA Ops:
  8.0 85.0 %all-gather.4.cloned.1.call-start = ((), (), s32[]{:S(2)}) async-start(), calls=%async_computation.2 | async-start | bytes 1064960 | tf_op jit(solution)/shard_map/all_gather | solution.py:80
  9.4 262.2 %all-reduce.7.cloned.1.call-start = ((), (), s32[]{:S(2)}) async-start(), calls=%async_computation.7 | async-start | bytes 1048576 | tf_op jit(solution)/shard_map/psum | solution.py:79
  13.5 329.6 %reduce-scatter.3.cloned.1.call-start = ((), (), s32[]{:S(2)}) async-start(), calls=%async_computation.3 | async-start | bytes 2129920 | tf_op jit(solution)/shard_map/reduce_scatter | solution.py:109
  100.7 6.7 copy-start.4
  107.5 8.4 %copy-start.7 = (s32[1,1,1,2]{3,2,1,0:T(1,128)S(1)}, s32[1,1,1,2]{3,2,1,0:T(1,128)}, u32[]{:S(2)}) copy-start(s32[1,1,1,2]{3,2,1,0:T(1,128)} %get-tuple-element.85) | copy-start | bytes 28 | tf_op jit(solution)/shard_map/cond
  121.7 302.8 %copy-start.1 = (s32[64]{0:T(128)S(1)}, s32[64]{0:T(128)}, u32[]{:S(2)}) copy-start(s32[64]{0:T(128)} %param.25) | copy-start | bytes 772
  121.8 375.7 %all-gather.6.cloned.1.call-start = ((), (), s32[]{:S(2)}) async-start(), calls=%async_computation.6 | async-start | bytes 1064960 | tf_op jit(solution)/shard_map/all_gather | solution.py:116
  271.6 227.7 %copy-start.2 = (s32[1,1,1,2]{3,2,1,0:T(1,128)S(1)}, s32[1,1,1,2]{3,2,1,0:T(1,128)}, u32[]{:S(2)}) copy-start(s32[1,1,1,2]{3,2,1,0:T(1,128)} %param.23) | copy-start | bytes 28
  271.6 227.7 %copy-start.3 = (s32[1,1,1,2]{3,2,1,0:T(1,128)S(1)}, s32[1,1,1,2]{3,2,1,0:T(1,128)}, u32[]{:S(2)}) copy-start(s32[1,1,1,2]{3,2,1,0:T(1,128)} %param.22) | copy-start | bytes 28
  271.6 227.7 %copy-start.6 = (s32[1,1,1,2]{3,2,1,0:T(1,128)S(1)}, s32[1,1,1,2]{3,2,1,0:T(1,128)}, u32[]{:S(2)}) copy-start(s32[1,1,1,2]{3,2,1,0:T(1,128)} %param.21) | copy-start | bytes 28
  424.5 253.1 %all-reduce.5.cloned.1.call-start = ((), (), s32[]{:S(2)}) async-start(), calls=%async_computation.4 | async-start | bytes 524288 | tf_op jit(solution)/shard_map/psum | solution.py:115
  425.8 313.4 %reduce-scatter.5.cloned.1.call-start = ((), (), s32[]{:S(2)}) async-start(), calls=%async_computation.5 | async-start | bytes 2129920 | tf_op jit(solution)/shard_map/reduce_scatter | solution.py:143
  523.1 154.5 %copy-start = (f32[256,256]{0,1:T(8,128)S(1)}, f32[256,256]{0,1:T(8,128)}, u32[]{:S(2)}) copy-start(f32[256,256]{0,1:T(8,128)} %get-tuple-element.143) | copy-start | bytes 786436
Sparse Core Ops, SparseCore 0:
  12.2 80.7 all-gather.3
  121.9 159.1 reduce-scatter.2
  424.6 72.8 all-gather.5
  527.0 159.5 reduce-scatter.4
Sparse Core Ops, SparseCore 1:
  15.6 256.0 all-reduce.6
  431.3 246.2 all-reduce.4
where the time goes:
time: 837 us; the launch traced here: 827 us
  waiting for transfers between devices  448 us (54%)
  blocking collectives  155 us (19%)
  other arithmetic  133 us (16%)
  local copies, waits for them, and re-layouts  42.5 us (5%)
  between operations  19.3 us (2%)
  matrix products  17.4 us (2%)
  loops' own time  12.2 us (1%)
    psum x1, waiting for transfers between devices, body(): gram_a = lax.psum(local_a, ('ia', 'ja', 'ka'))  151 us
    psum x1, waiting for transfers between devices, body(): gram_b, gram_c = lax.psum((local_b, local_c), ('ia', 'ja', 'ka'))  150 us
    psum x1, blocking collectives, body(): squares_a = lax.psum(jnp.sum(a_hat * a_hat, axis=0), ('ia', 'ja', 'ka'))  77.9 us
    psum x1, blocking collectives, body(): squares_b = lax.psum(jnp.sum(b_hat * b_hat, axis=0), ('ia', 'ja', 'ka'))  77.3 us
    all_gather x1, waiting for transfers between devices, body(): lax.all_gather(factor_b.astype(jnp.bfloat16), ('ia', 'ka'), axis=1, tiled...  75.5 us
    all_gather x1, waiting for transfers between devices, body(): lax.all_gather(a_own.astype(jnp.bfloat16)[None], ('ja', 'ka'), axis=1, ti...  71.7 us
    another operation x13, other arithmetic, solve_rows(): lower = jnp.linalg.cholesky(gram)  68.6 us
    another operation x5, other arithmetic, solve_rows(): return jax.scipy.linalg.cho_solve((lower, True), rows.T).T  39.4 us
  transfers between devices with their start and end apart: 6, of which 4 were waited for; matrix products, arithmetic and copies ran while one was open for 22% of the time, Pallas kernels for 0%

commit v1 on v0

--- a/solution.py
+++ b/solution.py
@@ -142,7 +142,8 @@
     stored_two = to_stored(partial_two, owner_two, piece_rows)
     summed_two = lax.psum_scatter(stored_two, ("ia", "ka"), scatter_dimension=0, tiled=True)
     b_hat = solve_rows(gram_a * gram_c, summed_two)
-    squares_b = lax.psum(jnp.sum(b_hat * b_hat, axis=0), ("ia", "ja", "ka"))
+    one_axis = lax.psum(jnp.sum(b_hat * b_hat, axis=0), ("ja", "ka"))
+    squares_b = lax.psum(one_axis, "ia")
     b_own = b_hat / jnp.sqrt(squares_b / total_one + EPS)
     return (a_own[None], b_own[None])
 

time: 837 us -> 896 us (1.070)
  blocking collectives: 155 us -> 211 us
    psum x1 -> x2, blocking collectives: 77.3 us -> 133 us  [the longest x1 126 us: body(): one_axis = lax.psum(jnp.sum(b_hat * b_hat, axis=0), ('ja', 'ka'))]
  transfers between devices with their start and end apart: 6 -> 6, of which waited for: 4 -> 4; matrix products, arithmetic and copies ran while one was open for 22% -> 21% of each run, Pallas kernels for 0% -> 0%
where the time goes in v1:
time: 896 us; the launch traced here: 884 us
  waiting for transfers between devices  448 us (50%)
  blocking collectives  211 us (24%)
  other arithmetic  133 us (15%)
  local copies, waits for them, and re-layouts  42.5 us (5%)
  between operations  19.3 us (2%)
  matrix products  17.4 us (2%)
  loops' own time  12.2 us (1%)
    psum x1, waiting for transfers between devices, body(): gram_a = lax.psum(local_a, ('ia', 'ja', 'ka'))  151 us
    psum x1, waiting for transfers between devices, body(): gram_b, gram_c = lax.psum((local_b, local_c), ('ia', 'ja', 'ka'))  150 us
    psum x1, blocking collectives, body(): one_axis = lax.psum(jnp.sum(b_hat * b_hat, axis=0), ('ja', 'ka'))  126 us
    psum x1, blocking collectives, body(): squares_a = lax.psum(jnp.sum(a_hat * a_hat, axis=0), ('ia', 'ja', 'ka'))  77.9 us
    all_gather x1, waiting for transfers between devices, body(): lax.all_gather(factor_b.astype(jnp.bfloat16), ('ia', 'ka'), axis=1, tiled...  75.5 us
    all_gather x1, waiting for transfers between devices, body(): lax.all_gather(a_own.astype(jnp.bfloat16)[None], ('ja', 'ka'), axis=1, ti...  71.7 us
    another operation x13, other arithmetic, solve_rows(): lower = jnp.linalg.cholesky(gram)  68.6 us
    another operation x5, other arithmetic, solve_rows(): return jax.scipy.linalg.cho_solve((lower, True), rows.T).T  39.4 us
  transfers between devices with their start and end apart: 6, of which 4 were waited for; matrix products, arithmetic and copies ran while one was open for 21% of the time, Pallas kernels for 0%

profile of v1, /device:TPU:1, one launch (start us, length us, event | category | flops | bytes accessed | tf_op | source)
XLA Modules:
  0.0 883.6 jit_solution(3957081961751890873)
XLA Ops:
  17.5 75.5 %all-gather.4.cloned.1.call-done = bf16[1,2048,256]{2,1,0:T(8,128)(2,1)} async-done(((bf16[1,32,256]{2,1,0:T(8,128)(2,1)}), bf16[1,2048,256]{2,1,0:T(8,128)(2,1)}) %all-gather.4.cloned.1.call-update) | async-done | bytes 1048592 | tf_op jit(solution)/shard_map/all_gather | solution.py:80
  94.8 23.3 %conditional.4 = (f32[2048,256]{1,0:T(8,128)}) conditional(s32[]{:T(128)} %bitcast.41, () %tuple.54, (s32[1,1,1,2]{3,2,1,0:T(1,128)}, bf16[512,256]{1,0:T(8,128)(2,1)S(1)}, bf16[1,1,1,2,128,128,128]{6,5,4,3,2,1,0:T(8,128)(2,1)}, s32[1,1,1,2]{3,2,1,0:T(1,128)}, bf16[2048,256]{1,0:T(8,128)(2,1)S(1)}, /*index=5*/s32[1,1,1,2]{3,2,1,0:T(1,128)}) %tuple.134), branch_computations={%region_6.0_spmd, %region_7.0_spmd} | conditional | flops 1082130432 | bytes 83099928 | solution.py:104
  100.7 6.7 copy.52
  107.6 8.2 multiply_reduce_fusion
  122.1 149.6 %all-reduce.7.cloned.1.call-done = (f32[256,256]{0,1:T(8,128)}, f32[256,256]{0,1:T(8,128)}) async-done(((f32[256,256]{0,1:T(8,128)}, f32[256,256]{0,1:T(8,128)}), (f32[256,256]{0,1:T(8,128)}, f32[256,256]{0,1:T(8,128)})) %all-reduce.7.cloned.1.call-update) | async-done | bytes 524304 | tf_op jit(solution)/shard_map/psum | solution.py:79
  272.9 11.7 %cholesky.130 = f32[128,128]{1,0:T(8,128)S(1)} custom-call(f32[128,128]{1,0:T(8,128)S(1)} %cholesky.194), custom_call_target="Cholesky" | custom-call | tf_op jit(solution)/shard_map/jit(cholesky)/cholesky | solution.py:10
  284.7 9.8 %custom-call.15 = f32[1,128,128]{1,2,0:T(8,128)S(1)} custom-call(f32[1,128,128]{2,1,0:T(8,128)S(1)} %get-tuple-element.155), custom_call_target="InvertDiagBlocksLowerTriangular" | custom-call | tf_op jit(solution)/shard_map/jit(cholesky)/cholesky | solution.py:10
  295.0 11.7 %cholesky.147 = f32[128,128]{1,0:T(8,128)S(1)} custom-call(f32[128,128]{1,0:T(8,128)S(1)} %convolution_subtract_fusion.1), custom_call_target="Cholesky" | custom-call | tf_op jit(solution)/shard_map/jit(cholesky)/cholesky | solution.py:10
  308.8 14.6 %while.4 = (s32[]{:T(128)}, f32[256,256]{1,0:T(8,128)S(1)}, s32[2,2]{1,0:T(2,128)S(1)}, f32[2,128,128]{2,1,0:T(8,128)S(1)}, s32[]{:T(128)}) while((s32[]{:T(128)}, f32[256,256]{1,0:T(8,128)S(1)}, s32[2,2]{1,0:T(2,128)S(1)}, f32[2,128,128]{2,1,0:T(8,128)S(1)}, s32[]{:T(128)}) %tuple.103), condition=%wide.while_cond, body=%wide.while_body.sunk | while | flops 2 | bytes 131181 | solution.py:11
  323.4 19.7 %custom-call.16 = f32[2,128,128]{1,2,0:T(8,128)S(1)} custom-call(f32[2,128,128]{2,1,0:T(8,128)S(1)} %get-tuple-element.124), custom_call_target="InvertDiagBlocksLowerTriangular" | custom-call | tf_op jit(solution)/shard_map/jit(_cho_solve)/triangular_solve | solution.py:11
  345.9 77.9 %psum.44 = f32[256]{0:T(256)S(1)} all-reduce(f32[256]{0:T(256)S(1)} %multiply_reduce_fusion.5), channel_id=1, replica_groups=mesh['ia'=4,'ja'=4,'ka'=16] {'ia','ja','ka'}, use_global_device_ids=true, to_apply=%region_13.16 | all-reduce | flops 256 | bytes 2048 | tf_op jit(solution)/shard_map/psum | solution.py:111
  425.8 71.7 %all-gather.6.cloned.1.call-done = bf16[2048,256]{1,0:T(8,128)(2,1)} async-done(((bf16[32,256]{1,0:T(8,128)(2,1)}), bf16[2048,256]{1,0:T(8,128)(2,1)}) %all-gather.6.cloned.1.call-update) | async-done | bytes 1048592 | tf_op jit(solution)/shard_map/all_gather | solution.py:116
  499.4 23.6 %conditional.6 = (f32[2048,256]{1,0:T(8,128)}) conditional(s32[]{:T(128)} %bitcast.41, () %tuple.57, (s32[1,1,1,2]{3,2,1,0:T(1,128)S(1)}, bf16[2048,256]{1,0:T(8,128)(2,1)S(1)}, bf16[1,1,1,2,128,128,128]{6,5,4,3,2,1,0:T(8,128)(2,1)}, s32[1,1,1,2]{3,2,1,0:T(1,128)S(1)}, bf16[512,256]{1,0:T(8,128)(2,1)S(1)}, ...), branch_computations={%region_15.18_spmd, %region_16.19_spmd} | conditional | flops 1082130432 | bytes 83099800 | solution.py:139
  505.5 6.7 copy.55
  512.4 8.3 multiply_reduce_fusion.2
  523.1 3.7 gather_fusion.3
  526.8 150.8 %all-reduce.5.cloned.1.call-done = f32[256,256]{0,1:T(8,128)} async-done(((f32[256,256]{0,1:T(8,128)}), f32[256,256]{0,1:T(8,128)}) %all-reduce.5.cloned.1.call-update) | async-done | bytes 262160 | tf_op jit(solution)/shard_map/psum | solution.py:115
  678.8 11.7 %cholesky.164 = f32[128,128]{1,0:T(8,128)S(1)} custom-call(f32[128,128]{1,0:T(8,128)S(1)} %cholesky.197), custom_call_target="Cholesky" | custom-call | tf_op jit(solution)/shard_map/jit(cholesky)/cholesky | solution.py:10
  690.6 9.8 %custom-call.17 = f32[1,128,128]{1,2,0:T(8,128)S(1)} custom-call(f32[1,128,128]{2,1,0:T(8,128)S(1)} %get-tuple-element.151), custom_call_target="InvertDiagBlocksLowerTriangular" | custom-call | tf_op jit(solution)/shard_map/jit(cholesky)/cholesky | solution.py:10
  700.9 11.7 %cholesky.181 = f32[128,128]{1,0:T(8,128)S(1)} custom-call(f32[128,128]{1,0:T(8,128)S(1)} %convolution_subtract_fusion), custom_call_target="Cholesky" | custom-call | tf_op jit(solution)/shard_map/jit(cholesky)/cholesky | solution.py:10
  715.2 4.2 while.5
  719.4 19.7 %custom-call.18 = f32[2,128,128]{1,2,0:T(8,128)S(1)} custom-call(f32[2,128,128]{2,1,0:T(8,128)S(1)} %get-tuple-element.125), custom_call_target="InvertDiagBlocksLowerTriangular" | custom-call | tf_op jit(solution)/shard_map/jit(_cho_solve)/triangular_solve | solution.py:11
  742.0 125.6 %psum.46 = f32[256]{0:T(256)S(1)} all-reduce(f32[256]{0:T(256)S(1)} %multiply_reduce_fusion.4), channel_id=1, replica_groups=mesh['ia'=4,'ja'=4,'ka'=16] {'ja','ka'}, use_global_device_ids=true, to_apply=%region_22.25 | all-reduce | flops 256 | bytes 2048 | tf_op jit(solution)/shard_map/psum | solution.py:145
  867.5 7.9 psum.47
  (118 shorter events, 54.1 us)
Async XLA Ops:
  8.0 85.0 %all-gather.4.cloned.1.call-start = ((), (), s32[]{:S(2)}) async-start(), calls=%async_computation.2 | async-start | bytes 1064960 | tf_op jit(solution)/shard_map/all_gather | solution.py:80
  9.4 262.2 %all-reduce.7.cloned.1.call-start = ((), (), s32[]{:S(2)}) async-start(), calls=%async_computation.7 | async-start | bytes 1048576 | tf_op jit(solution)/shard_map/psum | solution.py:79
  13.5 329.6 %reduce-scatter.3.cloned.1.call-start = ((), (), s32[]{:S(2)}) async-start(), calls=%async_computation.3 | async-start | bytes 2129920 | tf_op jit(solution)/shard_map/reduce_scatter | solution.py:109
  100.7 6.7 copy-start.4
  107.5 8.4 copy-start.7
  121.7 302.8 %copy-start.1 = (s32[64]{0:T(128)S(1)}, s32[64]{0:T(128)}, u32[]{:S(2)}) copy-start(s32[64]{0:T(128)} %param.25) | copy-start | bytes 772
  121.8 375.7 %all-gather.6.cloned.1.call-start = ((), (), s32[]{:S(2)}) async-start(), calls=%async_computation.6 | async-start | bytes 1064960 | tf_op jit(solution)/shard_map/all_gather | solution.py:116
  271.6 227.7 %copy-start.2 = (s32[1,1,1,2]{3,2,1,0:T(1,128)S(1)}, s32[1,1,1,2]{3,2,1,0:T(1,128)}, u32[]{:S(2)}) copy-start(s32[1,1,1,2]{3,2,1,0:T(1,128)} %param.23) | copy-start | bytes 28
  271.6 227.7 %copy-start.3 = (s32[1,1,1,2]{3,2,1,0:T(1,128)S(1)}, s32[1,1,1,2]{3,2,1,0:T(1,128)}, u32[]{:S(2)}) copy-start(s32[1,1,1,2]{3,2,1,0:T(1,128)} %param.22) | copy-start | bytes 28
  271.6 227.7 %copy-start.6 = (s32[1,1,1,2]{3,2,1,0:T(1,128)S(1)}, s32[1,1,1,2]{3,2,1,0:T(1,128)}, u32[]{:S(2)}) copy-start(s32[1,1,1,2]{3,2,1,0:T(1,128)} %param.21) | copy-start | bytes 28
  424.5 253.1 %all-reduce.5.cloned.1.call-start = ((), (), s32[]{:S(2)}) async-start(), calls=%async_computation.4 | async-start | bytes 524288 | tf_op jit(solution)/shard_map/psum | solution.py:115
  425.8 313.4 %reduce-scatter.5.cloned.1.call-start = ((), (), s32[]{:S(2)}) async-start(), calls=%async_computation.5 | async-start | bytes 2129920 | tf_op jit(solution)/shard_map/reduce_scatter | solution.py:143
  523.1 154.5 %copy-start = (f32[256,256]{0,1:T(8,128)S(1)}, f32[256,256]{0,1:T(8,128)}, u32[]{:S(2)}) copy-start(f32[256,256]{0,1:T(8,128)} %get-tuple-element.143) | copy-start | bytes 786436
Sparse Core Ops, SparseCore 0:
  12.2 80.7 all-gather.3
  121.9 159.1 reduce-scatter.2
  424.6 72.8 all-gather.5
  527.0 159.5 reduce-scatter.4
Sparse Core Ops, SparseCore 1:
  15.6 256.0 all-reduce.6
  431.3 246.2 all-reduce.4
